TPU v7x, 32 devices: a whole 2x2x4 slice. The times are simulated.
32 devices in a mesh: row: 8 (over z, core), col: 4 (over y, x).
Axes of the slice: x: 2, y: 2, z: 4, core: 2. Of those that a mesh axis runs over, the one named last changes fastest.
Arguments:
- matrix: float32 [12288, 12288], P('row', 'col'), may hold values from -8 to 8
Outputs:
- updated: float32 [12288, 12288], P('row', 'col')
- reflectors: float32 [16, 12288], replicated
- coefficients: float32 [2, 16], replicated
All inputs are finite; a program needn't handle non-finite values.
Results may differ from a plain program's by a relative error of at most 0.0003.
Values sent between devices are 32-bit elements; how exact they have to be, the bound alone decides.
A program may use at most 64 MiB of HBM per device.

v0:
```python
import jax
import jax.numpy as jnp
from jax import lax
from jax.sharding import PartitionSpec as P

PANEL_COLUMNS = 16


HIGH = lax.Precision.HIGHEST


def from_root(value, axis, source):
    kept = jnp.where(lax.axis_index(axis) == source, value, 0).astype(value.dtype)
    return lax.psum(kept, axis)


def per_device(matrix):
    tile_rows, tile_cols = matrix.shape
    order = tile_rows * lax.axis_size("row")
    row_start = lax.axis_index("row") * tile_rows
    col_start = lax.axis_index("col") * tile_cols
    panel = from_root(jnp.transpose(matrix[:, :PANEL_COLUMNS]), "col", 0)
    whole_panel = lax.all_gather(panel, "row", axis=1, tiled=True)
    everywhere = jnp.arange(order, dtype=jnp.int32)

    def single_column(step, loop_carry_state):
        reflectors, reflected_images, reflector_scales, below_diagonal = loop_carry_state
        local_reflectors = lax.dynamic_slice_in_dim(reflectors, row_start, tile_rows, 1)
        local_images = lax.dynamic_slice_in_dim(reflected_images, row_start, tile_rows, 1)
        reflector_entries = lax.dynamic_index_in_dim(reflectors, step, 1, False)
        image_entries = lax.dynamic_index_in_dim(reflected_images, step, 1, False)
        column_now = lax.dynamic_index_in_dim(whole_panel, step, 0, False)
        full_column = (
            column_now
            - jnp.dot(image_entries, reflectors, precision=HIGH)
            - jnp.dot(reflector_entries, reflected_images, precision=HIGH)
        )
        below = jnp.where(everywhere > step, full_column, 0.0)
        leading = lax.dynamic_index_in_dim(full_column, step + 1, 0, False)
        norm_value = jnp.sqrt(jnp.sum(below * below))
        reflector = jnp.where(everywhere == step + 1, 1.0, below / (leading + norm_value))
        reflector_scale = 1.0 + leading / norm_value
        reflector_cols = lax.dynamic_slice_in_dim(reflector, col_start, tile_cols, 0)
        images_dot = jnp.dot(reflected_images, reflector, precision=HIGH)
        reflect_dot = jnp.dot(reflectors, reflector, precision=HIGH)
        product = lax.psum(jnp.dot(matrix, reflector_cols, precision=HIGH), "col")
        local_image = reflector_scale * (
            product
            - jnp.dot(images_dot, local_reflectors, precision=HIGH)
            - jnp.dot(reflect_dot, local_images, precision=HIGH)
        )
        image = lax.all_gather(local_image, "row", axis=0, tiled=True)
        image = image - 0.5 * reflector_scale * jnp.sum(image * reflector) * reflector
        reflectors = reflectors.at[step].set(reflector)
        reflected_images = reflected_images.at[step].set(image)
        reflector_scales = reflector_scales.at[step].set(reflector_scale)
        below_diagonal = below_diagonal.at[step].set(-norm_value)
        return (reflectors, reflected_images, reflector_scales, below_diagonal)

    initial_state = (
        jnp.zeros((PANEL_COLUMNS, order), jnp.float32),
        jnp.zeros((PANEL_COLUMNS, order), jnp.float32),
        jnp.zeros((PANEL_COLUMNS,), jnp.float32),
        jnp.zeros((PANEL_COLUMNS,), jnp.float32),
    )
    reflectors, reflected_images, reflector_scales, below_diagonal = lax.fori_loop(
        0, PANEL_COLUMNS, single_column, initial_state
    )
    left_side = jnp.concatenate(
        [
            lax.dynamic_slice_in_dim(reflectors, row_start, tile_rows, 1),
            lax.dynamic_slice_in_dim(reflected_images, row_start, tile_rows, 1),
        ],
        axis=0,
    )
    right_side = jnp.concatenate(
        [
            lax.dynamic_slice_in_dim(reflected_images, col_start, tile_cols, 1),
            lax.dynamic_slice_in_dim(reflectors, col_start, tile_cols, 1),
        ],
        axis=0,
    )
    updated = matrix - jnp.einsum("kr,kc->rc", left_side, right_side, precision=HIGH)
    return (updated, reflectors, jnp.stack([reflector_scales, below_diagonal]))


def solution(mesh):
    placed = (P("row", "col"),)
    return jax.shard_map(
        per_device,
        mesh=mesh,
        in_specs=placed,
        out_specs=(P("row", "col"), P(), P()),
        check_vma=False,
    )
```

profile of v0, /device:TPU:0, one launch (start us, length us, event | category | flops | bytes accessed | tf_op | source)
XLA Modules:
  0.0 970.7 jit_solution(1444257417858805585)
XLA Ops:
  9.3 46.9 %all-reduce.2.cloned.1.call-done = f32[16,1536]{1,0:T(8,128)} async-done(((f32[16,1536]{1,0:T(8,128)}), f32[16,1536]{1,0:T(8,128)}) %all-reduce.2.cloned.1.call-update) | async-done | bytes 98320 | tf_op jit(solution)/shard_map/psum | solution.py:14
  56.3 15.7 %all_gather.13 = f32[16,12288]{1,0:T(8,128)S(1)} all-gather(f32[16,1536]{1,0:T(8,128)} %all-reduce.2.cloned.1.call-done), channel_id=1, replica_groups=mesh['row'=8,'col'=4] {'row'}, dimensions={1}, use_global_device_ids=true | all-gather | bytes 884736 | tf_op jit(solution)/shard_map/all_gather | solution.py:23
  72.1 870.5 %while.27 = (s32[]{:T(128)}, f32[16,12288]{1,0:T(8,128)S(1)}, f32[16,12288]{1,0:T(8,128)S(1)}, f32[16]{0:T(128)S(1)}, f32[16]{0:T(128)S(1)}, /*index=5*/f32[16,1...) while((s32[]{:T(128)}, f32[16,12288]{1,0:T(8,128)S(1)}, ...), condition=%wide.region_6.7_spmd.clone.clone, body=%wide.region_1.6_spmd.clone.clone.sunk | while | flops 66988052 | bytes 23705756 | solution.py:66
  72.1 1.5 and_reduce_fusion.2
  80.7 18.3 %convolution_reduce_fusion.7 = f32[1536]{0:T(1024)S(1)} fusion(f32[3072,1]{0,1:T(1,128)S(1)} %bitcast.100, f32[1536,3072]{1,0:T(8,128)} %get-tuple-element.526), kind=kOutput, calls=%fused_computation.3.clone.1 | convolution fusion | flops 56623104 | bytes 18892800 | tf_op jit(solution)/shard_map/while/body/eval_jaxpr/dot_general | solution.py:46
  99.0 9.1 psum.25
  108.2 14.0 %all-gather.3 = f32[8,1,1536]{2,1,0:T(1,128)S(1)} all-gather(f32[1,1,1536]{2,1,0:T(1,128)S(1)} %reshape.222), channel_id=1, replica_groups=mesh['row'=8,'col'=4] {'row'}, dimensions={0}, use_global_device_ids=true | all-gather | bytes 55296 | tf_op jit(solution)/shard_map/while/body/eval_jaxpr/all_gather | solution.py:52
  126.7 1.5 and_reduce_fusion.2
  135.4 18.3 %convolution_reduce_fusion.7 = f32[1536]{0:T(1024)S(1)} fusion(f32[3072,1]{0,1:T(1,128)S(1)} %bitcast.100, f32[1536,3072]{1,0:T(8,128)} %get-tuple-element.526), kind=kOutput, calls=%fused_computation.3.clone.1 | convolution fusion | flops 56623104 | bytes 18892800 | tf_op jit(solution)/shard_map/while/body/eval_jaxpr/dot_general | solution.py:46
  153.7 8.9 psum.25
  162.7 14.0 %all-gather.3 = f32[8,1,1536]{2,1,0:T(1,128)S(1)} all-gather(f32[1,1,1536]{2,1,0:T(1,128)S(1)} %reshape.222), channel_id=1, replica_groups=mesh['row'=8,'col'=4] {'row'}, dimensions={0}, use_global_device_ids=true | all-gather | bytes 55296 | tf_op jit(solution)/shard_map/while/body/eval_jaxpr/all_gather | solution.py:52
  181.3 1.5 and_reduce_fusion.2
  189.9 18.3 %convolution_reduce_fusion.7 = f32[1536]{0:T(1024)S(1)} fusion(f32[3072,1]{0,1:T(1,128)S(1)} %bitcast.100, f32[1536,3072]{1,0:T(8,128)} %get-tuple-element.526), kind=kOutput, calls=%fused_computation.3.clone.1 | convolution fusion | flops 56623104 | bytes 18892800 | tf_op jit(solution)/shard_map/while/body/eval_jaxpr/dot_general | solution.py:46
  208.2 9.1 psum.25
  217.4 14.0 %all-gather.3 = f32[8,1,1536]{2,1,0:T(1,128)S(1)} all-gather(f32[1,1,1536]{2,1,0:T(1,128)S(1)} %reshape.222), channel_id=1, replica_groups=mesh['row'=8,'col'=4] {'row'}, dimensions={0}, use_global_device_ids=true | all-gather | bytes 55296 | tf_op jit(solution)/shard_map/while/body/eval_jaxpr/all_gather | solution.py:52
  236.0 1.5 and_reduce_fusion.2
  244.6 18.3 %convolution_reduce_fusion.7 = f32[1536]{0:T(1024)S(1)} fusion(f32[3072,1]{0,1:T(1,128)S(1)} %bitcast.100, f32[1536,3072]{1,0:T(8,128)} %get-tuple-element.526), kind=kOutput, calls=%fused_computation.3.clone.1 | convolution fusion | flops 56623104 | bytes 18892800 | tf_op jit(solution)/shard_map/while/body/eval_jaxpr/dot_general | solution.py:46
  262.9 8.1 psum.25
  271.1 14.0 %all-gather.3 = f32[8,1,1536]{2,1,0:T(1,128)S(1)} all-gather(f32[1,1,1536]{2,1,0:T(1,128)S(1)} %reshape.222), channel_id=1, replica_groups=mesh['row'=8,'col'=4] {'row'}, dimensions={0}, use_global_device_ids=true | all-gather | bytes 55296 | tf_op jit(solution)/shard_map/while/body/eval_jaxpr/all_gather | solution.py:52
  289.7 1.5 and_reduce_fusion.2
  298.3 18.3 %convolution_reduce_fusion.7 = f32[1536]{0:T(1024)S(1)} fusion(f32[3072,1]{0,1:T(1,128)S(1)} %bitcast.100, f32[1536,3072]{1,0:T(8,128)} %get-tuple-element.526), kind=kOutput, calls=%fused_computation.3.clone.1 | convolution fusion | flops 56623104 | bytes 18892800 | tf_op jit(solution)/shard_map/while/body/eval_jaxpr/dot_general | solution.py:46
  316.6 9.1 psum.25
  325.8 14.0 %all-gather.3 = f32[8,1,1536]{2,1,0:T(1,128)S(1)} all-gather(f32[1,1,1536]{2,1,0:T(1,128)S(1)} %reshape.222), channel_id=1, replica_groups=mesh['row'=8,'col'=4] {'row'}, dimensions={0}, use_global_device_ids=true | all-gather | bytes 55296 | tf_op jit(solution)/shard_map/while/body/eval_jaxpr/all_gather | solution.py:52
  344.4 1.5 and_reduce_fusion.2
  353.1 18.3 %convolution_reduce_fusion.7 = f32[1536]{0:T(1024)S(1)} fusion(f32[3072,1]{0,1:T(1,128)S(1)} %bitcast.100, f32[1536,3072]{1,0:T(8,128)} %get-tuple-element.526), kind=kOutput, calls=%fused_computation.3.clone.1 | convolution fusion | flops 56623104 | bytes 18892800 | tf_op jit(solution)/shard_map/while/body/eval_jaxpr/dot_general | solution.py:46
  371.4 8.8 psum.25
  380.2 14.0 %all-gather.3 = f32[8,1,1536]{2,1,0:T(1,128)S(1)} all-gather(f32[1,1,1536]{2,1,0:T(1,128)S(1)} %reshape.222), channel_id=1, replica_groups=mesh['row'=8,'col'=4] {'row'}, dimensions={0}, use_global_device_ids=true | all-gather | bytes 55296 | tf_op jit(solution)/shard_map/while/body/eval_jaxpr/all_gather | solution.py:52
  398.8 1.5 and_reduce_fusion.2
  407.5 18.3 %convolution_reduce_fusion.7 = f32[1536]{0:T(1024)S(1)} fusion(f32[3072,1]{0,1:T(1,128)S(1)} %bitcast.100, f32[1536,3072]{1,0:T(8,128)} %get-tuple-element.526), kind=kOutput, calls=%fused_computation.3.clone.1 | convolution fusion | flops 56623104 | bytes 18892800 | tf_op jit(solution)/shard_map/while/body/eval_jaxpr/dot_general | solution.py:46
  425.8 9.2 psum.25
  435.0 14.0 %all-gather.3 = f32[8,1,1536]{2,1,0:T(1,128)S(1)} all-gather(f32[1,1,1536]{2,1,0:T(1,128)S(1)} %reshape.222), channel_id=1, replica_groups=mesh['row'=8,'col'=4] {'row'}, dimensions={0}, use_global_device_ids=true | all-gather | bytes 55296 | tf_op jit(solution)/shard_map/while/body/eval_jaxpr/all_gather | solution.py:52
  453.6 1.5 and_reduce_fusion.2
  462.3 18.3 %convolution_reduce_fusion.7 = f32[1536]{0:T(1024)S(1)} fusion(f32[3072,1]{0,1:T(1,128)S(1)} %bitcast.100, f32[1536,3072]{1,0:T(8,128)} %get-tuple-element.526), kind=kOutput, calls=%fused_computation.3.clone.1 | convolution fusion | flops 56623104 | bytes 18892800 | tf_op jit(solution)/shard_map/while/body/eval_jaxpr/dot_general | solution.py:46
  480.6 8.1 psum.25
  488.7 14.0 %all-gather.3 = f32[8,1,1536]{2,1,0:T(1,128)S(1)} all-gather(f32[1,1,1536]{2,1,0:T(1,128)S(1)} %reshape.222), channel_id=1, replica_groups=mesh['row'=8,'col'=4] {'row'}, dimensions={0}, use_global_device_ids=true | all-gather | bytes 55296 | tf_op jit(solution)/shard_map/while/body/eval_jaxpr/all_gather | solution.py:52
  507.3 1.5 and_reduce_fusion.2
  516.0 18.3 %convolution_reduce_fusion.7 = f32[1536]{0:T(1024)S(1)} fusion(f32[3072,1]{0,1:T(1,128)S(1)} %bitcast.100, f32[1536,3072]{1,0:T(8,128)} %get-tuple-element.526), kind=kOutput, calls=%fused_computation.3.clone.1 | convolution fusion | flops 56623104 | bytes 18892800 | tf_op jit(solution)/shard_map/while/body/eval_jaxpr/dot_general | solution.py:46
  534.3 9.2 psum.25
  543.5 14.0 %all-gather.3 = f32[8,1,1536]{2,1,0:T(1,128)S(1)} all-gather(f32[1,1,1536]{2,1,0:T(1,128)S(1)} %reshape.222), channel_id=1, replica_groups=mesh['row'=8,'col'=4] {'row'}, dimensions={0}, use_global_device_ids=true | all-gather | bytes 55296 | tf_op jit(solution)/shard_map/while/body/eval_jaxpr/all_gather | solution.py:52
  562.1 1.5 and_reduce_fusion.2
  570.7 18.3 %convolution_reduce_fusion.7 = f32[1536]{0:T(1024)S(1)} fusion(f32[3072,1]{0,1:T(1,128)S(1)} %bitcast.100, f32[1536,3072]{1,0:T(8,128)} %get-tuple-element.526), kind=kOutput, calls=%fused_computation.3.clone.1 | convolution fusion | flops 56623104 | bytes 18892800 | tf_op jit(solution)/shard_map/while/body/eval_jaxpr/dot_general | solution.py:46
  589.0 8.8 psum.25
  597.9 14.0 %all-gather.3 = f32[8,1,1536]{2,1,0:T(1,128)S(1)} all-gather(f32[1,1,1536]{2,1,0:T(1,128)S(1)} %reshape.222), channel_id=1, replica_groups=mesh['row'=8,'col'=4] {'row'}, dimensions={0}, use_global_device_ids=true | all-gather | bytes 55296 | tf_op jit(solution)/shard_map/while/body/eval_jaxpr/all_gather | solution.py:52
  625.2 18.3 %convolution_reduce_fusion.7 = f32[1536]{0:T(1024)S(1)} fusion(f32[3072,1]{0,1:T(1,128)S(1)} %bitcast.100, f32[1536,3072]{1,0:T(8,128)} %get-tuple-element.526), kind=kOutput, calls=%fused_computation.3.clone.1 | convolution fusion | flops 56623104 | bytes 18892800 | tf_op jit(solution)/shard_map/while/body/eval_jaxpr/dot_general | solution.py:46
  643.5 9.2 psum.25
  652.6 14.0 %all-gather.3 = f32[8,1,1536]{2,1,0:T(1,128)S(1)} all-gather(f32[1,1,1536]{2,1,0:T(1,128)S(1)} %reshape.222), channel_id=1, replica_groups=mesh['row'=8,'col'=4] {'row'}, dimensions={0}, use_global_device_ids=true | all-gather | bytes 55296 | tf_op jit(solution)/shard_map/while/body/eval_jaxpr/all_gather | solution.py:52
  671.2 1.5 and_reduce_fusion.2
  679.9 18.3 %convolution_reduce_fusion.7 = f32[1536]{0:T(1024)S(1)} fusion(f32[3072,1]{0,1:T(1,128)S(1)} %bitcast.100, f32[1536,3072]{1,0:T(8,128)} %get-tuple-element.526), kind=kOutput, calls=%fused_computation.3.clone.1 | convolution fusion | flops 56623104 | bytes 18892800 | tf_op jit(solution)/shard_map/while/body/eval_jaxpr/dot_general | solution.py:46
  698.2 8.1 psum.25
  706.4 14.0 %all-gather.3 = f32[8,1,1536]{2,1,0:T(1,128)S(1)} all-gather(f32[1,1,1536]{2,1,0:T(1,128)S(1)} %reshape.222), channel_id=1, replica_groups=mesh['row'=8,'col'=4] {'row'}, dimensions={0}, use_global_device_ids=true | all-gather | bytes 55296 | tf_op jit(solution)/shard_map/while/body/eval_jaxpr/all_gather | solution.py:52
  733.6 18.3 %convolution_reduce_fusion.7 = f32[1536]{0:T(1024)S(1)} fusion(f32[3072,1]{0,1:T(1,128)S(1)} %bitcast.100, f32[1536,3072]{1,0:T(8,128)} %get-tuple-element.526), kind=kOutput, calls=%fused_computation.3.clone.1 | convolution fusion | flops 56623104 | bytes 18892800 | tf_op jit(solution)/shard_map/while/body/eval_jaxpr/dot_general | solution.py:46
  751.9 9.2 psum.25
  761.1 14.0 %all-gather.3 = f32[8,1,1536]{2,1,0:T(1,128)S(1)} all-gather(f32[1,1,1536]{2,1,0:T(1,128)S(1)} %reshape.222), channel_id=1, replica_groups=mesh['row'=8,'col'=4] {'row'}, dimensions={0}, use_global_device_ids=true | all-gather | bytes 55296 | tf_op jit(solution)/shard_map/while/body/eval_jaxpr/all_gather | solution.py:52
  788.4 18.3 %convolution_reduce_fusion.7 = f32[1536]{0:T(1024)S(1)} fusion(f32[3072,1]{0,1:T(1,128)S(1)} %bitcast.100, f32[1536,3072]{1,0:T(8,128)} %get-tuple-element.526), kind=kOutput, calls=%fused_computation.3.clone.1 | convolution fusion | flops 56623104 | bytes 18892800 | tf_op jit(solution)/shard_map/while/body/eval_jaxpr/dot_general | solution.py:46
  806.7 8.8 psum.25
  815.5 14.0 %all-gather.3 = f32[8,1,1536]{2,1,0:T(1,128)S(1)} all-gather(f32[1,1,1536]{2,1,0:T(1,128)S(1)} %reshape.222), channel_id=1, replica_groups=mesh['row'=8,'col'=4] {'row'}, dimensions={0}, use_global_device_ids=true | all-gather | bytes 55296 | tf_op jit(solution)/shard_map/while/body/eval_jaxpr/all_gather | solution.py:52
  842.8 18.3 %convolution_reduce_fusion.7 = f32[1536]{0:T(1024)S(1)} fusion(f32[3072,1]{0,1:T(1,128)S(1)} %bitcast.100, f32[1536,3072]{1,0:T(8,128)} %get-tuple-element.526), kind=kOutput, calls=%fused_computation.3.clone.1 | convolution fusion | flops 56623104 | bytes 18892800 | tf_op jit(solution)/shard_map/while/body/eval_jaxpr/dot_general | solution.py:46
  861.1 9.2 psum.25
  870.3 14.0 %all-gather.3 = f32[8,1,1536]{2,1,0:T(1,128)S(1)} all-gather(f32[1,1,1536]{2,1,0:T(1,128)S(1)} %reshape.222), channel_id=1, replica_groups=mesh['row'=8,'col'=4] {'row'}, dimensions={0}, use_global_device_ids=true | all-gather | bytes 55296 | tf_op jit(solution)/shard_map/while/body/eval_jaxpr/all_gather | solution.py:52
  888.9 1.5 and_reduce_fusion.2
  897.6 18.3 %convolution_reduce_fusion.7 = f32[1536]{0:T(1024)S(1)} fusion(f32[3072,1]{0,1:T(1,128)S(1)} %bitcast.100, f32[1536,3072]{1,0:T(8,128)} %get-tuple-element.526), kind=kOutput, calls=%fused_computation.3.clone.1 | convolution fusion | flops 56623104 | bytes 18892800 | tf_op jit(solution)/shard_map/while/body/eval_jaxpr/dot_general | solution.py:46
  915.9 8.1 psum.25
  924.0 14.0 %all-gather.3 = f32[8,1,1536]{2,1,0:T(1,128)S(1)} all-gather(f32[1,1,1536]{2,1,0:T(1,128)S(1)} %reshape.222), channel_id=1, replica_groups=mesh['row'=8,'col'=4] {'row'}, dimensions={0}, use_global_device_ids=true | all-gather | bytes 55296 | tf_op jit(solution)/shard_map/while/body/eval_jaxpr/all_gather | solution.py:52
  943.4 20.5 %convolution_subtract_fusion = f32[1536,3072]{1,0:T(8,128)} fusion(f32[1536,3072]{1,0:T(8,128)} %get-tuple-element.536, f32[16,3072]{1,0:T(8,128)S(1)} %get-tuple-element.420, f32[16,3072]{1,0:T(8,128)S(1)} %get-tuple-element.421, f32[16,1536]{1,0:T(8,128)S(1)} %get-tuple-element.422, f32[16,1536]{1,0:T(8,128)S(1)} %get-tuple-element.423), kind=kOutput, calls=%fused_computation.32 | convolution fusion | flops 1816805376 | bytes 38338560 | tf_op jit(solution)/shard_map/kr,kc->rc/dot_general | solution.py:83
  (370 shorter events, 156.2 us)
Async XLA Ops:
  7.2 49.1 %all-reduce.2.cloned.1.call-start = ((), (), s32[]{:S(2)}) async-start(), calls=%async_computation | async-start | bytes 196608 | tf_op jit(solution)/shard_map/psum | solution.py:14
  942.6 21.2 %copy-start = (f32[16,12288]{1,0:T(8,128)}, f32[16,12288]{1,0:T(8,128)S(1)}, u32[]{:S(2)}) copy-start(f32[16,12288]{1,0:T(8,128)S(1)} %get-tuple-element.396) | copy-start | bytes 2359300
Sparse Core Ops, SparseCore 0:
  11.4 44.7 all-reduce.1
where the time goes:
time: 972 us; the launch traced here: 971 us
  blocking collectives  381 us (39%)
  matrix products  368 us (38%)
  other arithmetic  73.9 us (8%)
  waiting for transfers between devices  47 us (5%)
  local copies, waits for them, and re-layouts  44.9 us (5%)
  loops' own time  41.4 us (4%)
  between operations  14.1 us (1%)
    dot_general x16, matrix products, single_column(): product = lax.psum(jnp.dot(matrix, reflector_cols, precision=HIGH), 'col')  293 us
    all_gather x16, blocking collectives, single_column(): image = lax.all_gather(local_image, 'row', axis=0, tiled=True)  225 us
    psum x16, blocking collectives, single_column(): product = lax.psum(jnp.dot(matrix, reflector_cols, precision=HIGH), 'col')  141 us
    another operation x48, other arithmetic  47.2 us
    psum x1, waiting for transfers between devices, from_root(): return lax.psum(kept, axis)  46.9 us
    another operation x1, loops' own time, per_device(): lax.fori_loop(0, PANEL_COLUMNS, single_column, initial_state)  41.4 us
    dot_general x1, matrix products, per_device(): jnp.einsum('kr,kc->rc', left_side, right_side, precision=HIGH)  20.5 us
  transfers between devices with their start and end apart: 1, of which 1 were waited for; matrix products, arithmetic and copies ran while one was open for 0% of the time, Pallas kernels for 0%

commit v1 on v0

v1 whole, which is shorter than its diff:
```python
import jax
import jax.numpy as jnp
from jax import lax
from jax.experimental import pallas as pl
from jax.experimental.pallas import tpu as pltpu
from jax.sharding import PartitionSpec as P

K = 16
HEAD = 24
LANES = 128
MESH = pl.DeviceIdType.MESH


def lane_pick(block, lanes, index):
    return jnp.sum(jnp.where(lanes == index, block, 0.0), axis=1, keepdims=True)


def panel_kernel(rows, cols, n_row, n_col, mat, v_out, wc_out, vw_out, coef_out, kap_out,
                 tile, panel, vw, msg, recv, gout, c0_ref, u_ref, p_ref, au_ref, b0_ref,
                 vu_ref, wu_ref, s_ref, kmsg, krecv,
                 load_sem, panel_sem, psend_sem, send_sem, recv_sem, gsend_sem, v_sem, w_sem,
                 ksend_sem, k_sem):
    width = rows + LANES
    halves = cols // rows
    r = lax.axis_index("row")
    c = lax.axis_index("col")
    blocks = rows // LANES
    ctiles = cols // LANES

    def chunk(i):
        part = pl.ds(pl.multiple_of(i * LANES, LANES), LANES)
        return pltpu.make_async_copy(mat.at[part], tile.at[part], load_sem.at[i])

    def start_chunk(i, carry):
        chunk(i).start()
        return carry

    barrier = pltpu.get_barrier_semaphore()
    for dr in range(n_row):
        for dc in range(n_col):
            if dr or dc:
                pl.semaphore_signal(barrier, inc=1, device_id=(lax.rem(r + dr, n_row), lax.rem(c + dc, n_col)),
                                    device_id_type=MESH)
    vw[...] = jnp.zeros_like(vw)
    u_ref[...] = jnp.zeros_like(u_ref)
    p_ref[...] = jnp.zeros_like(p_ref)
    au_ref[...] = jnp.zeros_like(au_ref)
    vu_ref[...] = jnp.zeros_like(vu_ref)
    wu_ref[...] = jnp.zeros_like(wu_ref)
    s_ref[...] = jnp.zeros_like(s_ref)
    coef_out[...] = jnp.zeros_like(coef_out)
    pl.semaphore_wait(barrier, n_row * n_col - 1)

    def panel_copy(h, dc, local):
        src = mat.at[0:HEAD, h * rows:(h + 1) * rows]
        dst = panel.at[:, 0:rows]
        if local:
            return pltpu.make_async_copy(src, dst, panel_sem)
        return pltpu.make_async_remote_copy(
            src, dst, psend_sem, panel_sem,
            device_id=(halves * c + h, lax.rem(c + dc, n_col)), device_id_type=MESH)

    def head_copy(dr, dc, local):
        src = mat.at[0:HEAD, 0:LANES]
        dst = panel.at[:, rows:width]
        if local:
            return pltpu.make_async_copy(src, dst, panel_sem)
        return pltpu.make_async_remote_copy(src, dst, psend_sem, panel_sem, device_id=(dr, dc), device_id_type=MESH)

    def each_target(fn_remote, fn_local):
        for dc in range(n_col):
            for h in range(halves):
                if dc:
                    fn_remote(h, dc)
                else:
                    own = halves * c + h == r
                    pl.when(jnp.logical_not(own))(lambda h=h, dc=dc: fn_remote(h, dc))
                    if fn_local is not None:
                        pl.when(own)(lambda h=h, dc=dc: fn_local(h, dc))

    @pl.when(r == 0)
    def _():
        @pl.when(c == 0)
        def _():
            for dr in range(n_row):
                for dc in range(n_col):
                    head_copy(dr, dc, dr == 0 and dc == 0).start()
        each_target(lambda h, dc: panel_copy(h, dc, False).start(), lambda h, dc: panel_copy(h, dc, True).start())

    lax.fori_loop(0, blocks, start_chunk, 0)
    pltpu.make_async_copy(panel, panel, panel_sem).wait()

    @pl.when(r == 0)
    def _():
        @pl.when(c == 0)
        def _():
            for dr in range(n_row):
                for dc in range(n_col):
                    if dr or dc:
                        head_copy(dr, dc, False).wait_send()
        each_target(lambda h, dc: panel_copy(h, dc, False).wait_send(), None)

    c0_ref[...] = panel[0:1, :]
    lane = lax.broadcasted_iota(jnp.int32, (1, width), 1)
    pos = jnp.where(lane < rows, lane + r * rows, jnp.where(lane < rows + HEAD, lane - rows, -1))
    l128 = lax.broadcasted_iota(jnp.int32, (1, LANES), 1)
    k16 = lax.broadcasted_iota(jnp.int32, (K, 1), 0)

    def send_copy(j, h, dc, local):
        src = msg.at[j, h]
        dst = recv.at[j, r]
        if local:
            return pltpu.make_async_copy(src, dst, recv_sem.at[j])
        return pltpu.make_async_remote_copy(
            src, dst, send_sem, recv_sem.at[j],
            device_id=(halves * c + h, lax.rem(c + dc, n_col)), device_id_type=MESH)

    def v_copy(j, dr):
        return pltpu.make_async_remote_copy(
            gout.at[j, 0], v_out.at[j, r], gsend_sem, v_sem,
            device_id=(lax.rem(r + dr, n_row), c), device_id_type=MESH)

    def w_copy(j, dr):
        return pltpu.make_async_remote_copy(
            gout.at[j, 1], wc_out.at[j, lax.rem(r, halves)], gsend_sem, w_sem,
            device_id=(lax.rem(r + dr, n_row), c), device_id_type=MESH)

    def k_copy(dr):
        return pltpu.make_async_remote_copy(
            kmsg, krecv.at[r], ksend_sem, k_sem,
            device_id=(lax.rem(r + dr, n_row), c), device_id_type=MESH)

    gives_w = r // halves == c

    def spread(i):
        row = b0_ref[:, pl.ds(pl.multiple_of(i * LANES, LANES), LANES)]
        return jnp.broadcast_to(row, (LANES, LANES)).T

    def step(j, carry):
        m2 = pos > j + 1
        c0 = c0_ref[...]
        b0 = jnp.where(m2, c0, 0.0)
        b0_ref[...] = b0
        u_prev = u_ref[...]
        p_prev = p_ref[...]

        b_loc = b0[:, :rows]
        dvw = jnp.sum(vw[:, :rows] * b_loc, axis=1, keepdims=True)
        dpn = jnp.sum(panel[:, :rows] * b_loc, axis=1, keepdims=True)
        n0 = jnp.sum(b_loc * b_loc, axis=1, keepdims=True)
        kp = jnp.sum(u_prev[:, :rows] * p_prev[:, :rows], axis=1, keepdims=True)
        s32 = lax.broadcasted_iota(jnp.int32, (2 * K, LANES), 0)
        t32 = lax.broadcasted_iota(jnp.int32, (2 * K, LANES), 1)
        s24 = lax.broadcasted_iota(jnp.int32, (HEAD, LANES), 0)
        t24 = lax.broadcasted_iota(jnp.int32, (HEAD, LANES), 1)
        sc = jnp.sum(jnp.where(s32 == t32, dvw, 0.0), axis=0, keepdims=True)
        sc += jnp.sum(jnp.where(s24 + 2 * K == t24, dpn, 0.0), axis=0, keepdims=True)
        sc += jnp.where(l128 == 2 * K + HEAD, n0, 0.0) + jnp.where(l128 == 2 * K + HEAD + 1, kp, 0.0)

        def block(i, state):
            bc, accs = state
            pl.when(j == 0)(lambda: chunk(i).wait())
            nxt = spread(jnp.minimum(i + 1, blocks - 1))
            b3 = bc.reshape(LANES // 8, 8, LANES)
            part = pl.ds(pl.multiple_of(i * LANES, LANES), LANES)
            new = []
            for t in range(ctiles):
                x = tile[part, t * LANES:(t + 1) * LANES].reshape(LANES // 8, 8, LANES)
                new.append(accs[t] + jnp.sum(x * b3, axis=0))
            return nxt, tuple(new)

        zero = jnp.zeros((8, LANES), jnp.float32)
        _, accs = lax.fori_loop(0, blocks, block, (spread(0), (zero,) * ctiles))
        per = rows // LANES
        for h in range(halves):
            for t in range(per):
                msg[j, h, :, t * LANES:(t + 1) * LANES] = jnp.sum(accs[h * per + t], axis=0, keepdims=True)
            msg[j, h, :, rows:width] = sc

        each_target(lambda h, dc: send_copy(j, h, dc, False).start(), lambda h, dc: send_copy(j, h, dc, True).start())
        pltpu.make_async_copy(recv.at[j], recv.at[j], recv_sem.at[j]).wait()

        tot = jnp.sum(recv[j], axis=0)
        sc = tot[:, rows:width]
        wide = jnp.broadcast_to(sc, (2 * K, LANES))
        dots = jnp.sum(jnp.where(s32 == t32, wide, 0.0), axis=1, keepdims=True)
        n0 = sc[:, 2 * K + HEAD:2 * K + HEAD + 1]
        kp = sc[:, 2 * K + HEAD + 1:2 * K + HEAD + 2]
        tau_prev = s_ref[0:1, 0:1]
        bb_prev = s_ref[1:2, 0:1]
        kap = 0.5 * tau_prev * kp
        kap_out[pl.ds(j, 1), :] = jnp.broadcast_to(kap, (1, LANES))
        vw[pl.ds(K + j - 1, 1), :] = p_prev - kap * u_prev
        pj = panel[pl.ds(j, 1), :]
        pj1 = panel[pl.ds(j + 1, 1), :]
        col = c0 + 2.0 * kap * u_prev
        uj1 = lane_pick(u_prev[:, rows:width], l128, j + 1)
        aq = au_ref[...] - pj - uj1 * pj1
        yhead = jnp.where(l128 < HEAD, pltpu.roll(sc, LANES - 2 * K, 1), 0.0)
        y = jnp.concatenate([tot[:, :rows], yhead], axis=1) + 2.0 * kap * aq
        vb = dots[:K]
        wb = dots[K:]
        last = k16 == j - 1
        n1 = jnp.sum(jnp.where(last, vb, 0.0), axis=0, keepdims=True)
        b2 = jnp.maximum(n0 + 4.0 * kap * (n1 + kap * (bb_prev - uj1 * uj1)), 0.0)
        lead = lane_pick(col[:, rows:width], l128, j + 1)
        sig = jnp.sqrt(b2 + lead * lead)
        inv = 1.0 / (lead + sig)
        tau = 1.0 + lead / sig
        u = jnp.where(m2, col * inv, 0.0) + jnp.where(pos == j + 1, 1.0, 0.0)
        au = y * inv + pj1

        head = vw[:, rows:width]
        hj = lane_pick(head, l128, j)
        hj1 = lane_pick(head, l128, j + 1)
        uu = bb_prev + 1.0
        vup = jnp.where(last, uu, vu_ref[:, 0:1])
        wup = jnp.where(last, kp - kap * uu, wu_ref[:, 0:1])
        wb = jnp.where(last, wb - kap * vb, wb)
        vu = (vb + 2.0 * kap * (vup - hj[:K] - uj1 * hj1[:K])) * inv + hj1[:K]
        wu = (wb + 2.0 * kap * (wup - hj[K:] - uj1 * hj1[K:])) * inv + hj1[K:]
        v_all = vw[0:K, :]
        w_all = vw[K:2 * K, :]
        p = tau * (au - jnp.sum(v_all * wu + w_all * vu, axis=0, keepdims=True))
        pj1_entry = lane_pick(p[:, rows:width], l128, j + 1)
        c0n = pj1 - jnp.sum(v_all * hj1[K:] + w_all * hj1[:K], axis=0, keepdims=True) - pj1_entry * u - p
        gout[j, 0] = u[:, :rows]
        gout[j, 1] = p[:, :rows]
        c0_ref[...] = c0n
        u_ref[...] = u
        p_ref[...] = p
        au_ref[...] = au
        vu_ref[...] = jnp.broadcast_to(vu, (K, LANES))
        wu_ref[...] = jnp.broadcast_to(wu, (K, LANES))
        s_ref[0:1, :] = jnp.broadcast_to(tau, (1, LANES))
        s_ref[1:2, :] = jnp.broadcast_to(b2 * inv * inv, (1, LANES))
        coef_out[0:1, :] = jnp.where(l128 == j, tau, coef_out[0:1, :])
        coef_out[1:2, :] = jnp.where(l128 == j, -sig, coef_out[1:2, :])
        vw[pl.ds(j, 1), :] = u
        vw[pl.ds(K + j, 1), :] = p

        for dr in range(1, n_row):
            v_copy(j, dr).start()
        pltpu.make_async_copy(gout.at[j, 0], v_out.at[j, r], v_sem).start()

        @pl.when(gives_w)
        def _():
            for dr in range(1, n_row):
                w_copy(j, dr).start()
            pltpu.make_async_copy(gout.at[j, 1], wc_out.at[j, lax.rem(r, halves)], w_sem).start()
        return carry

    lax.fori_loop(0, K, step, 0)

    u = u_ref[...]
    p = p_ref[...]
    kp = jnp.sum(u[:, :rows] * p[:, :rows], axis=1, keepdims=True)
    kmsg[...] = jnp.broadcast_to(kp, (1, LANES))
    for dr in range(1, n_row):
        k_copy(dr).start()
    pltpu.make_async_copy(kmsg, krecv.at[r], k_sem).start()
    pltpu.make_async_copy(krecv, krecv, k_sem).wait()
    kap = 0.5 * s_ref[0:1, :] * jnp.sum(krecv[...], axis=0)
    kap_out[K:K + 1, :] = kap
    vw[2 * K - 1:2 * K, :] = p - kap[:, 0:1] * u
    vw_out[...] = vw[:, :rows]

    def drain(j, carry):
        each_target(lambda h, dc: send_copy(j, h, dc, False).wait_send(), None)
        for dr in range(1, n_row):
            v_copy(j, dr).wait_send()

        @pl.when(gives_w)
        def _():
            for dr in range(1, n_row):
                w_copy(j, dr).wait_send()
        return carry

    lax.fori_loop(0, K, drain, 0)
    for dr in range(1, n_row):
        k_copy(dr).wait_send()
    pltpu.make_async_copy(v_out, v_out, v_sem).wait()
    pltpu.make_async_copy(wc_out, wc_out, w_sem).wait()


def pieces(x):
    hi = lax.reduce_precision(x, 8, 7)
    rest = x - hi
    mid = lax.reduce_precision(rest, 8, 7)
    low = lax.reduce_precision(rest - mid, 8, 7)
    return [part.astype(jnp.bfloat16) for part in (hi, mid, low)]


def make_per_device(n_row, n_col):
    def per_device(matrix):
        rows, cols = matrix.shape
        halves = cols // rows
        width = rows + LANES
        f32 = jnp.float32
        vmem = pl.BlockSpec(memory_space=pltpu.VMEM)
        anyspace = pl.BlockSpec(memory_space=pl.ANY)
        dma = pltpu.SemaphoreType.DMA

        def kernel(*refs):
            panel_kernel(rows, cols, n_row, n_col, *refs)

        v_full, wc, vw, coef, kap = pl.pallas_call(
            kernel,
            out_shape=(
                jax.ShapeDtypeStruct((K, n_row, 1, rows), f32),
                jax.ShapeDtypeStruct((K, halves, 1, rows), f32),
                jax.ShapeDtypeStruct((2 * K, rows), f32),
                jax.ShapeDtypeStruct((2, LANES), f32),
                jax.ShapeDtypeStruct((K + 1, LANES), f32),
            ),
            in_specs=[anyspace],
            out_specs=(anyspace, anyspace, vmem, vmem, vmem),
            scratch_shapes=[
                pltpu.VMEM((rows, cols), f32),
                pltpu.VMEM((HEAD, width), f32),
                pltpu.VMEM((2 * K, width), f32),
                pltpu.VMEM((K, halves, 1, width), f32),
                pltpu.VMEM((K, n_row, 1, width), f32),
                pltpu.VMEM((K, 2, 1, rows), f32),
                pltpu.VMEM((1, width), f32),
                pltpu.VMEM((1, width), f32),
                pltpu.VMEM((1, width), f32),
                pltpu.VMEM((1, width), f32),
                pltpu.VMEM((1, width), f32),
                pltpu.VMEM((K, LANES), f32),
                pltpu.VMEM((K, LANES), f32),
                pltpu.VMEM((8, LANES), f32),
                pltpu.VMEM((1, LANES), f32),
                pltpu.VMEM((n_row, 1, LANES), f32),
                dma((rows // LANES,)),
                dma, dma, dma,
                dma((K,)),
                dma, dma, dma, dma, dma,
            ],
            compiler_params=pltpu.CompilerParams(
                collective_id=0, has_side_effects=True, vmem_limit_bytes=48 * 1024 * 1024),
        )(matrix)
        reflectors = v_full.reshape(K, n_row * rows)
        c = lax.axis_index("col")
        v_cols = lax.dynamic_slice_in_dim(reflectors, c * cols, cols, 1)
        w_cols = wc.reshape(K, cols) - kap[1:, 0:1] * v_cols
        left = pieces(vw)
        right = pieces(jnp.concatenate([w_cols, v_cols], axis=0))
        order = ((0, 0), (0, 1), (1, 0), (1, 1), (0, 2), (2, 0))
        big_left = jnp.concatenate([left[a] for a, _ in order], axis=0)
        big_right = jnp.concatenate([right[b] for _, b in order], axis=0)
        change = lax.dot_general(big_left, big_right, (((0,), (0,)), ((), ())), preferred_element_type=f32)
        return matrix - change, reflectors, coef[:, :K]
    return per_device


def solution(mesh):
    return jax.shard_map(
        make_per_device(mesh.shape["row"], mesh.shape["col"]),
        mesh=mesh,
        in_specs=(P("row", "col"),),
        out_specs=(P("row", "col"), P(), P()),
        check_vma=False,
    )
```

time: 972 us -> 169 us (0.17)
  blocking collectives: 381 us -> 0 us
  matrix products: 368 us -> 12.1 us
  Pallas kernels: 0 us -> 151 us
  other arithmetic: 73.9 us -> 2.86 us
  waiting for transfers between devices: 47 us -> 0 us
  local copies, waits for them, and re-layouts: 44.9 us -> 1.69 us
  loops' own time: 41.4 us -> 0 us
  between operations: 14.1 us -> 0.77 us
    dot_general x113 -> x1, matrix products: 368 us -> 12.1 us  [per_device(): lax.dot_general(big_left, big_right, (((0,), (0,)), ((), ())), preferred_...]
    all_gather x17 -> x0, blocking collectives: 240 us -> none  [the longest x16 225 us: single_column(): image = lax.all_gather(local_image, 'row', axis=0, tiled=True)]
    pallas_call x0 -> x1, Pallas kernels: none -> 151 us  [per_device(): pl.pallas_call(kernel, out_shape=(jax.ShapeDtypeStruct((K, n_row, 1, rows...]
    psum x16 -> x0, blocking collectives: 141 us -> none  [single_column(): product = lax.psum(jnp.dot(matrix, reflector_cols, precision=HIGH), 'col')]
    another operation x49 -> x0, other arithmetic: 47.9 us -> none
    psum x1 -> x0, waiting for transfers between devices: 46.9 us -> none  [from_root(): return lax.psum(kept, axis)]
    another operation x1 -> x0, loops' own time: 41.4 us -> none  [per_device(): lax.fori_loop(0, PANEL_COLUMNS, single_column, initial_state)]
    scatter x32 -> x0, local copies, waits for them, and re-layouts: 28.9 us -> none  [the longest x16 14.5 us: single_column(): reflectors = reflectors.at[step].set(reflector)]
  transfers between devices with their start and end apart: 1 -> 0, of which waited for: 1 -> 0; matrix products, arithmetic and copies ran while one was open for 0% -> 0% of each run, Pallas kernels for 0% -> 0%
where the time goes in v1:
time: 169 us; the launch traced here: 168 us
  Pallas kernels  151 us (89%)
  matrix products  12.1 us (7%)
  other arithmetic  2.86 us (2%)
  local copies, waits for them, and re-layouts  1.69 us (1%)
    pallas_call x1, Pallas kernels, per_device(): pl.pallas_call(kernel, out_shape=(jax.ShapeDtypeStruct((K, n_row, 1, rows...  151 us
    dot_general x1, matrix products, per_device(): lax.dot_general(big_left, big_right, (((0,), (0,)), ((), ())), preferred_...  12.1 us

profile of v1, /device:TPU:0, one launch (start us, length us, event | category | flops | bytes accessed | tf_op | source)
XLA Modules:
  0.0 168.5 jit_solution(12299380327796701054)
XLA Ops:
  0.6 151.0 %shard_map.38 = (f32[16,8,1,1536]{3,2,1,0:T(1,128)S(1)}, f32[16,2,1,1536]{3,2,1,0:T(1,128)S(1)}, f32[32,1536]{1,0:T(8,128)S(1)}, f32[2,128]{1,0:T(2,128)S(1)}, f32[17,128]{1,0:T(8,128)S(1)}) custom-call(f32[1536,3072]{1,0:T(8,128)} %refs_0_.1), custom_call_target="tpu_custom_call" | custom-call | tf_op jit(solution)/shard_map/pallas_call | solution.py:307
  151.6 0.6 reduce
  152.2 1.9 %reduce.2 = f32[16,8,1536]{2,1,0:T(8,128)S(1)} reduce(f32[16,8,1,1536]{3,2,1,0:T(1,128)S(1)} %get-tuple-element.11, f32[]{:T(128)} %constant.10), dimensions={2}, to_apply=%get-tuple-element.11.reduce_sub_computation | reduce | bytes 1572868 | tf_op jit(solution)/shard_map/pallas_call | solution.py:307
  154.1 0.5 copy.5
  154.5 0.0 copy-start
  154.6 0.1 slice_reduce_fusion
  154.7 0.1 multiply_subtract_fusion
  154.9 0.5 copy-done
  155.6 0.1 fusion.4
  155.7 12.1 %convolution_subtract_fusion = f32[1536,3072]{1,0:T(8,128)} fusion(f32[1536,3072]{1,0:T(8,128)} %refs_0_.1, bf16[192,1536]{1,0:T(8,128)(2,1)S(1)} %fusion.5, bf16[192,3072]{1,0:T(8,128)(2,1)S(1)} %constant_dynamic-update-slice_fusion.5), kind=kOutput, calls=%fused_computation | convolution fusion | flops 1816657920 | bytes 39518208 | tf_op jit(solution)/shard_map/dot_general | solution.py:352
  167.9 0.6 copy.17
  (12 shorter events, 0.3 us)
Async XLA Ops:
  154.5 0.9 copy-start

commit v2 on v1

--- a/solution.py
+++ b/solution.py
@@ -16,9 +16,9 @@
 
 
 def panel_kernel(rows, cols, n_row, n_col, mat, v_out, wc_out, vw_out, coef_out, kap_out,
-                 tile, panel, vw, msg, recv, gout, c0_ref, u_ref, p_ref, au_ref, b0_ref,
+                 tile, first, panel, vw, msg, recv, gout, c0_ref, u_ref, p_ref, au_ref, b0_ref,
                  vu_ref, wu_ref, s_ref, kmsg, krecv,
-                 load_sem, panel_sem, psend_sem, send_sem, recv_sem, gsend_sem, v_sem, w_sem,
+                 load_sem, first_sem, panel_sem, head_sem, psend_sem, send_sem, recv_sem, gsend_sem, v_sem, w_sem,
                  ksend_sem, k_sem):
     width = rows + LANES
     halves = cols // rows
@@ -35,12 +35,24 @@
         chunk(i).start()
         return carry
 
+    first_copy = pltpu.make_async_copy(mat.at[:, 0:LANES], first, first_sem)
+    pl.when(c == 0)(lambda: first_copy.start())
+    lax.fori_loop(0, blocks, start_chunk, 0)
+
     barrier = pltpu.get_barrier_semaphore()
     for dr in range(n_row):
         for dc in range(n_col):
             if dr or dc:
                 pl.semaphore_signal(barrier, inc=1, device_id=(lax.rem(r + dr, n_row), lax.rem(c + dc, n_col)),
                                     device_id_type=MESH)
+
+    @pl.when(c == 0)
+    def _():
+        first_copy.wait()
+        for i in range(blocks):
+            part = slice(i * LANES, (i + 1) * LANES)
+            panel[:, part] = first[part, :].T[0:HEAD, :]
+
     vw[...] = jnp.zeros_like(vw)
     u_ref[...] = jnp.zeros_like(u_ref)
     p_ref[...] = jnp.zeros_like(p_ref)
@@ -51,21 +63,17 @@
     coef_out[...] = jnp.zeros_like(coef_out)
     pl.semaphore_wait(barrier, n_row * n_col - 1)
 
-    def panel_copy(h, dc, local):
-        src = mat.at[0:HEAD, h * rows:(h + 1) * rows]
-        dst = panel.at[:, 0:rows]
-        if local:
-            return pltpu.make_async_copy(src, dst, panel_sem)
-        return pltpu.make_async_remote_copy(
-            src, dst, psend_sem, panel_sem,
-            device_id=(halves * c + h, lax.rem(c + dc, n_col)), device_id_type=MESH)
-
-    def head_copy(dr, dc, local):
+    def panel_copy(dc):
+        return pltpu.make_async_remote_copy(
+            panel.at[:, 0:rows], panel.at[:, 0:rows], psend_sem, panel_sem,
+            device_id=(r, dc), device_id_type=MESH)
+
+    def head_copy(dr, dc):
         src = mat.at[0:HEAD, 0:LANES]
         dst = panel.at[:, rows:width]
-        if local:
-            return pltpu.make_async_copy(src, dst, panel_sem)
-        return pltpu.make_async_remote_copy(src, dst, psend_sem, panel_sem, device_id=(dr, dc), device_id_type=MESH)
+        if dr == 0 and dc == 0:
+            return pltpu.make_async_copy(src, dst, head_sem)
+        return pltpu.make_async_remote_copy(src, dst, psend_sem, head_sem, device_id=(dr, dc), device_id_type=MESH)
 
     def each_target(fn_remote, fn_local):
         for dc in range(n_col):
@@ -78,27 +86,21 @@
                     if fn_local is not None:
                         pl.when(own)(lambda h=h, dc=dc: fn_local(h, dc))
 
-    @pl.when(r == 0)
+    @pl.when(c == 0)
     def _():
-        @pl.when(c == 0)
+        @pl.when(r == 0)
         def _():
-            for dr in range(n_row):
-                for dc in range(n_col):
-                    head_copy(dr, dc, dr == 0 and dc == 0).start()
-        each_target(lambda h, dc: panel_copy(h, dc, False).start(), lambda h, dc: panel_copy(h, dc, True).start())
-
-    lax.fori_loop(0, blocks, start_chunk, 0)
-    pltpu.make_async_copy(panel, panel, panel_sem).wait()
-
-    @pl.when(r == 0)
+            for dr in reversed(range(n_row)):
+                for dc in reversed(range(n_col)):
+                    head_copy(dr, dc).start()
+        for dc in reversed(range(1, n_col)):
+            panel_copy(dc).start()
+
+    pltpu.make_async_copy(panel.at[:, rows:width], panel.at[:, rows:width], head_sem).wait()
+
+    @pl.when(c != 0)
     def _():
-        @pl.when(c == 0)
-        def _():
-            for dr in range(n_row):
-                for dc in range(n_col):
-                    if dr or dc:
-                        head_copy(dr, dc, False).wait_send()
-        each_target(lambda h, dc: panel_copy(h, dc, False).wait_send(), None)
+        pltpu.make_async_copy(panel.at[:, 0:rows], panel.at[:, 0:rows], panel_sem).wait()
 
     c0_ref[...] = panel[0:1, :]
     lane = lax.broadcasted_iota(jnp.int32, (1, width), 1)
@@ -277,6 +279,18 @@
         return carry
 
     lax.fori_loop(0, K, drain, 0)
+
+    @pl.when(c == 0)
+    def _():
+        @pl.when(r == 0)
+        def _():
+            for dr in range(n_row):
+                for dc in range(n_col):
+                    if dr or dc:
+                        head_copy(dr, dc).wait_send()
+        for dc in range(1, n_col):
+            panel_copy(dc).wait_send()
+
     for dr in range(1, n_row):
         k_copy(dr).wait_send()
     pltpu.make_async_copy(v_out, v_out, v_sem).wait()
@@ -317,6 +331,7 @@
             out_specs=(anyspace, anyspace, vmem, vmem, vmem),
             scratch_shapes=[
                 pltpu.VMEM((rows, cols), f32),
+                pltpu.VMEM((rows, LANES), f32),
                 pltpu.VMEM((HEAD, width), f32),
                 pltpu.VMEM((2 * K, width), f32),
                 pltpu.VMEM((K, halves, 1, width), f32),
@@ -333,7 +348,7 @@
                 pltpu.VMEM((1, LANES), f32),
                 pltpu.VMEM((n_row, 1, LANES), f32),
                 dma((rows // LANES,)),
-                dma, dma, dma,
+                dma, dma, dma, dma, dma,
                 dma((K,)),
                 dma, dma, dma, dma, dma,
             ],

time: 169 us -> 161 us (0.953)
  Pallas kernels: 151 us -> 143 us
    pallas_call x1, Pallas kernels: 151 us -> 143 us  [per_device(): pl.pallas_call(kernel, out_shape=(jax.ShapeDtypeStruct((K, n_row, 1, rows...]
where the time goes in v2:
time: 161 us
  Pallas kernels  143 us (89%)
  matrix products  12.1 us (8%)
  other arithmetic  2.86 us (2%)
  local copies, waits for them, and re-layouts  1.69 us (1%)
    pallas_call x1, Pallas kernels, per_device(): pl.pallas_call(kernel, out_shape=(jax.ShapeDtypeStruct((K, n_row, 1, rows...  143 us
    dot_general x1, matrix products, per_device(): lax.dot_general(big_left, big_right, (((0,), (0,)), ((), ())), preferred_...  12.1 us

profile of v2, /device:TPU:0, one launch (start us, length us, event | category | flops | bytes accessed | tf_op | source)
XLA Modules:
  0.0 160.9 jit_solution(1245821992768311875)
XLA Ops:
  0.6 143.4 %shard_map.38 = (f32[16,8,1,1536]{3,2,1,0:T(1,128)S(1)}, f32[16,2,1,1536]{3,2,1,0:T(1,128)S(1)}, f32[32,1536]{1,0:T(8,128)S(1)}, f32[2,128]{1,0:T(2,128)S(1)}, f32[17,128]{1,0:T(8,128)S(1)}) custom-call(f32[1536,3072]{1,0:T(8,128)} %refs_0_.1), custom_call_target="tpu_custom_call" | custom-call | tf_op jit(solution)/shard_map/pallas_call | solution.py:321
  144.0 0.6 reduce
  144.6 1.9 %reduce.2 = f32[16,8,1536]{2,1,0:T(8,128)S(1)} reduce(f32[16,8,1,1536]{3,2,1,0:T(1,128)S(1)} %get-tuple-element.11, f32[]{:T(128)} %constant.10), dimensions={2}, to_apply=%get-tuple-element.11.reduce_sub_computation | reduce | bytes 1572868 | tf_op jit(solution)/shard_map/pallas_call | solution.py:321
  146.5 0.5 copy.5
  147.0 0.0 copy-start
  147.0 0.1 slice_reduce_fusion
  147.1 0.1 multiply_subtract_fusion
  147.3 0.5 copy-done
  148.1 0.1 fusion.4
  148.2 12.1 %convolution_subtract_fusion = f32[1536,3072]{1,0:T(8,128)} fusion(f32[1536,3072]{1,0:T(8,128)} %refs_0_.1, bf16[192,1536]{1,0:T(8,128)(2,1)S(1)} %fusion.5, bf16[192,3072]{1,0:T(8,128)(2,1)S(1)} %constant_dynamic-update-slice_fusion.5), kind=kOutput, calls=%fused_computation | convolution fusion | flops 1816657920 | bytes 39518208 | tf_op jit(solution)/shard_map/dot_general | solution.py:367
  160.3 0.6 copy.17
  (12 shorter events, 0.3 us)
Async XLA Ops:
  147.0 0.9 copy-start
